TPU v7x, 128 devices: a whole 4x4x4 slice. The times are simulated.
128 devices in a mesh: gz: 64 (over y, z, x_lo, core), rows: 2 (over x_hi).
Axes of the slice: x: 4 (x_hi: 2, x_lo: 2; x = x_hi * 2 + x_lo), y: 4, z: 4, core: 2. Of those that a mesh axis runs over, the one named last changes fastest.
Arguments:
- unary_cost: bfloat16 [256, 8, 225, 512], P('gz', 'rows'), may hold values from -6 to 6
- descriptors: bfloat16 [256, 225, 256], P('gz'), may hold values from -0.25 to 0.25
- valid_rows: int32 [256, 8], P('gz', 'rows'), may hold values 0 or 1
- offsets: int32 [225, 2], replicated, may hold values from -7 to 7, as said below
Outputs:
- energy: float32 [256, 8, 225, 512], P('gz', 'rows')
- displacement: float32 [2, 256, 8, 512], P(None, 'gz', 'rows')
Inputs may be any that keep to these rules, and one draw needn't show every extreme that they name: `offsets`: each row is a distinct pair, and every pair of whole numbers from -(7) to 7 appears once.
All inputs are finite; a program needn't handle non-finite values. No bound on the sum of `valid_rows` on one device may be relied on, other than what follows from the above.
Results may differ from a plain program's by a relative error of at most 0.0032.
Values may be sent and summed in bfloat16 or wider, within the bound.
A program may use at most 128 MiB of HBM per device.

v0:
```python
import functools

import jax
import jax.numpy as jnp
from jax import lax
from jax.experimental import pallas as pl
from jax.experimental.pallas import tpu as pltpu
from jax.sharding import PartitionSpec as P

BF = jnp.bfloat16
F32 = jnp.float32
MESH = pl.DeviceIdType.MESH
LAB = 225
FEAT = 256
COLS = 512
SKIP = frozenset()


def kernel(n, data, desc, compat_in, off_in, out, disp, x, xr, m0, m0r, p0, p0r, p1, m1, dd, dt, compat, off, s_buf, ps_buf, stage, send, recv, load, store):
    d = lax.axis_index("gz")
    h = lax.axis_index("rows")
    par = lax.rem(d, 2)
    prev = lax.rem(d + n - 1, n)
    nxt = lax.rem(d + 1, n)
    other = 1 - h
    relay_to = lax.rem(d + n - 1 + 2 * par, n)
    swap_with = d + 1 - 2 * par
    r0 = 2 - 2 * h
    r_edge = 3 - 3 * h
    below = jnp.where(d > 0, 1.0, 0.0).astype(F32)
    above = jnp.where(d < n - 1, 1.0, 0.0).astype(F32)

    def row(q):
        return q + h * (3 - 2 * q)

    barrier = pltpu.get_barrier_semaphore()
    for g in (prev, nxt):
        for k in (h, other):
            pl.semaphore_signal(barrier, inc=1, device_id=(g, k), device_id_type=MESH)
    pl.semaphore_wait(barrier, 4)

    count = [0]

    def remote(src, dst, g, k):
        i = count[0]
        count[0] += 1
        return pltpu.make_async_remote_copy(src_ref=src, dst_ref=dst, send_sem=send.at[i], recv_sem=recv.at[i], device_id=(g, k), device_id_type=MESH)

    near_up = remote(data.at[:, pl.ds(2, 2)], x.at[:, pl.ds(2, 2)], nxt, h)
    near_dn = remote(data.at[:, pl.ds(0, 2)], x.at[:, pl.ds(8, 2)], prev, h)
    desc_up = remote(desc, dd.at[pl.ds(0, 4)], nxt, other)
    desc_dn = remote(desc, dd.at[pl.ds(8, 4)], prev, other)
    corner = remote(data.at[r_edge, pl.ds(2 * par, 2)], xr.at[other, pl.ds(6 - 6 * par, 2)], relay_to, other)
    edge_up = remote(data.at[pl.ds(r0, 2), pl.ds(0, 2)], x.at[pl.ds(r0, 2), pl.ds(0, 2)], nxt, h)
    edge_dn = remote(data.at[pl.ds(r0, 2), pl.ds(2, 2)], x.at[pl.ds(r0, 2), pl.ds(10, 2)], prev, h)
    far_up = remote(data.at[pl.ds(2 - r0, 2), pl.ds(0, 2)], x.at[pl.ds(2 - r0, 2), pl.ds(0, 2)], nxt, h)
    far_dn = remote(data.at[pl.ds(2 - r0, 2), pl.ds(2, 2)], x.at[pl.ds(2 - r0, 2), pl.ds(10, 2)], prev, h)
    relay_near = remote(x.at[pl.ds(r0, 2), pl.ds(2 + 6 * par, 2)], xr.at[:, pl.ds(4 - 2 * par, 2)], relay_to, other)
    relay_far = remote(x.at[pl.ds(r0, 2), pl.ds(10 * par, 2)], xr.at[:, pl.ds(2 + 2 * par, 2)], relay_to, other)
    swap = remote(xr.at[h, pl.ds(4 - 2 * par, 2)], xr.at[h, pl.ds(6 * par, 2)], swap_with, h)

    for c in (near_up, near_dn, desc_up, desc_dn, corner, edge_up, edge_dn, far_up, far_dn):
        c.start()
    loads = [
        pltpu.make_async_copy(data, x.at[:, pl.ds(4, 4)], load.at[0]),
        pltpu.make_async_copy(desc, dd.at[pl.ds(4, 4)], load.at[1]),
        pltpu.make_async_copy(compat_in, compat, load.at[2]),
        pltpu.make_async_copy(off_in, off, load.at[3]),
    ]
    for c in loads:
        c.start()
    for c in loads:
        c.wait()

    def loop(count_, body):
        lax.fori_loop(0, count_, lambda i, c: (body(i), c)[1], 0)

    def soft_to(src, dst, flag):
        for j in range(4):
            cols = pl.ds(128 * j, 128)
            w = jnp.exp(-src[:, cols].astype(F32))
            inv = flag / jnp.sum(w, axis=0, keepdims=True)
            dst[:, cols] = (w * inv).astype(BF)

    def flag_of(e):
        return jnp.where(e < 4, below, jnp.where(e > 7, above, 1.0))

    def transpose(e):
        dt[e] = jnp.transpose(dd[e].astype(F32)).astype(BF)

    def project(e, src, dst):
        dst[...] = jnp.dot(dt[e], src[...], preferred_element_type=F32).astype(BF)

    def first(r, e):
        soft_to(x.at[r, e], m0.at[r, e], flag_of(e))
        project(e, m0.at[r, e], p0.at[r, e])

    lane = lax.broadcasted_iota(jnp.int32, (LAB, COLS), 1)

    def gather(near, far, planes, centre):
        s = near[0][...].astype(F32) + near[1][...].astype(F32)
        s = s + 0.5 * (far[0][...].astype(F32) + far[1][...].astype(F32))
        for p in planes:
            s = s + p[...].astype(F32)
        c = centre[...].astype(F32)
        s = s + jnp.where(lane > 0, pltpu.roll(c, 1, 1), 0.0)
        s = s + jnp.where(lane < COLS - 1, pltpu.roll(c, COLS - 1, 1), 0.0)
        s_buf[...] = s.astype(BF)

    def gather_p(a, b, c, g, e):
        ps_buf[...] = (a[...].astype(F32) + b[...].astype(F32) + c[...].astype(F32) + g[...].astype(F32)).astype(BF)

    def energy_of(e, dref, cols):
        v = dref[:, cols].astype(F32)
        v = v + jnp.dot(compat[...], s_buf[:, cols], preferred_element_type=F32)
        return v + jnp.dot(dd[e], ps_buf[:, cols], preferred_element_type=F32)

    def norm(v, flag):
        w = jnp.exp(-v)
        inv = flag / jnp.sum(w, axis=0, keepdims=True)
        return (w * inv).astype(BF)

    def mz(r, e):
        return m0.at[r, e]

    def sweep1(q, e, dst):
        r = row(q)
        planes = []
        if q > 0:
            planes.append(m0.at[row(q - 1), e])
        planes.append(m0.at[row(q + 1), e] if q < 3 else m0r.at[e - 2])
        gather((mz(r, e - 1), mz(r, e + 1)), (mz(r, e - 2), mz(r, e + 2)), planes, mz(r, e))
        gather_p(p0.at[r, e - 1], p0.at[r, e + 1], p0.at[r, e - 2], p0.at[r, e + 2], e)
        for j in range(2):
            cols = pl.ds(256 * j, 256)
            dst[:, cols] = norm(energy_of(e, x.at[r, e], cols), flag_of(e))

    def sweep1_rim(e):
        t = e - 2
        gather((m0r.at[t - 1], m0r.at[t + 1]), (m0r.at[t - 2], m0r.at[t + 2]), [m0.at[row(3), e], m0r.at[8 + e - 4]], m0r.at[t])
        gather_p(p0r.at[t - 1], p0r.at[t + 1], p0r.at[t - 2], p0r.at[t + 2], e)
        for j in range(2):
            cols = pl.ds(256 * j, 256)
            m0r.at[8 + e - 4][:, cols] = norm(energy_of(e, xr.at[h, t], cols), 1.0)

    def m1_at(r, e):
        return x.at[r, e]

    def copy_out(r, k):
        return pltpu.make_async_copy(stage.at[k], out.at[k, :, r, :], store.at[k])

    def sweep2(q, first_use):
        r = row(q)

        def one(k):
            e = 4 + k
            planes = []
            if q > 0:
                planes.append(m1.at[row(q - 1), k])
            planes.append(m1.at[row(q + 1), k] if q < 3 else m0r.at[8 + k])
            gather(*NEIGH(r, k), planes, m1.at[r, k])
            if not first_use:
                copy_out(r, k).wait()
            for j in range(2):
                cols = pl.ds(256 * j, 256)
                v = energy_of(e, x.at[r, e], cols)
                stage.at[k][:, cols] = v
                disp.at[k, r][:, cols] = jnp.dot(off[...], norm(v, 1.0), preferred_element_type=F32)
            copy_out(r, k).start()

        def NEIGH(r, k):
            def at(e):
                return m1.at[r, e - 4] if 4 <= e < 8 else x.at[r, e]
            e = 4 + k
            pp = [p1.at[r, t - 2] for t in (e - 1, e + 1, e - 2, e + 2)]
            gather_p(*pp, e)
            return (at(e - 1), at(e + 1)), (at(e - 2), at(e + 2))

        for k in range(4):
            one(k)

    def project1(q, e):
        r = row(q)
        project(e, x.at[r, e], p1.at[r, e - 2])

    def project1_own(q, k):
        r = row(q)
        project(4 + k, m1.at[r, k], p1.at[r, 2 + k])

    def wing(i):
        return 2 + i + 4 * lax.div(i, 2)

    def tip(i):
        return i + 8 * lax.div(i, 2)

    loop(4, lambda i: transpose(4 + i))
    loop(16, lambda i: first(lax.div(i, 4), 4 + lax.rem(i, 4)))

    near_up.wait_recv()
    near_dn.wait_recv()
    relay_near.start()
    desc_up.wait_recv()
    desc_dn.wait_recv()
    loop(8, lambda i: transpose(i + 4 * lax.div(i, 4)))
    loop(16, lambda i: first(lax.div(i, 4), wing(lax.rem(i, 4))))
    for q in range(3):
        loop(4, lambda i: sweep1(q, 4 + i, m1.at[row(q), i]))
        loop(4, lambda i: project1_own(q, i))

    edge_up.wait_recv()
    edge_dn.wait_recv()
    relay_far.start()
    loop(8, lambda i: first(row(2 + lax.div(i, 4)), tip(lax.rem(i, 4))))

    corner.wait_recv()
    relay_near.wait()
    loop(4, lambda i: sweep1(2, wing(i), x.at[row(2), wing(i)]))
    loop(4, lambda i: project1(2, wing(i)))
    relay_far.wait_recv()
    swap.start()
    swap.wait_recv()

    def rim(t):
        soft_to(xr.at[h, t], m0r.at[t], flag_of(t + 2))
        project(t + 2, m0r.at[t], p0r.at[t])

    loop(8, rim)
    loop(4, lambda i: soft_to(xr.at[other, i + 2], m0r.at[8 + i], 1.0))
    loop(4, lambda i: sweep1_rim(4 + i))
    loop(4, lambda i: sweep1(3, 4 + i, m1.at[row(3), i]))
    loop(4, lambda i: project1_own(3, i))
    relay_far.wait_send()
    loop(4, lambda i: sweep1(3, wing(i), x.at[row(3), wing(i)]))
    loop(4, lambda i: project1(3, wing(i)))
    sweep2(3, True)
    sweep2(2, False)

    far_up.wait_recv()
    far_dn.wait_recv()
    loop(8, lambda i: first(row(lax.div(i, 4)), tip(lax.rem(i, 4))))
    for q in (1, 0):
        loop(4, lambda i: sweep1(q, wing(i), x.at[row(q), wing(i)]))
        loop(4, lambda i: project1(q, wing(i)))
        sweep2(q, False)
    for k in range(4):
        copy_out(row(0), k).wait()
    for c in (near_up, near_dn, desc_up, desc_dn, corner, edge_up, edge_dn, far_up, far_dn, swap):
        c.wait_send()


def on_device(n, unary_cost, descriptors, valid_rows, offsets):
    data = jnp.transpose(unary_cost, (1, 0, 2, 3)) * valid_rows.astype(BF).T[:, :, None, None]
    co = offsets.astype(F32)
    spread = jnp.abs(co[:, None, 0] - co[None, :, 0]) + jnp.abs(co[:, None, 1] - co[None, :, 1])
    compat = (0.125 * jnp.minimum(spread, 6.0)).astype(BF)
    off8 = jnp.concatenate([offsets.T, jnp.zeros((6, LAB), offsets.dtype)], axis=0).astype(BF)
    hbm = pl.BlockSpec(memory_space=pl.ANY)
    e, disp = pl.pallas_call(
        functools.partial(kernel, n),
        in_specs=[hbm] * 4,
        out_specs=[hbm, pl.BlockSpec(memory_space=pltpu.VMEM)],
        out_shape=[jax.ShapeDtypeStruct((4, LAB, 4, COLS), F32), jax.ShapeDtypeStruct((4, 4, 8, COLS), F32)],
        scratch_shapes=[
            pltpu.VMEM((4, 12, LAB, COLS), BF),
            pltpu.VMEM((2, 8, LAB, COLS), BF),
            pltpu.VMEM((4, 12, LAB, COLS), BF),
            pltpu.VMEM((12, LAB, COLS), BF),
            pltpu.VMEM((4, 12, FEAT, COLS), BF),
            pltpu.VMEM((8, FEAT, COLS), BF),
            pltpu.VMEM((4, 8, FEAT, COLS), BF),
            pltpu.VMEM((4, 4, LAB, COLS), BF),
            pltpu.VMEM((12, LAB, FEAT), BF),
            pltpu.VMEM((12, FEAT, LAB), BF),
            pltpu.VMEM((LAB, LAB), BF),
            pltpu.VMEM((8, LAB), BF),
            pltpu.VMEM((LAB, COLS), BF),
            pltpu.VMEM((FEAT, COLS), BF),
            pltpu.VMEM((4, LAB, COLS), F32),
            pltpu.SemaphoreType.DMA((12,)),
            pltpu.SemaphoreType.DMA((12,)),
            pltpu.SemaphoreType.DMA((4,)),
            pltpu.SemaphoreType.DMA((4,)),
        ],
        compiler_params=pltpu.CompilerParams(collective_id=0, has_side_effects=True, vmem_limit_bytes=67043328),
        name="mega",
    )(data, descriptors, compat, off8)
    return jnp.transpose(e, (0, 2, 1, 3)), jnp.transpose(disp[:, :, 0:2], (2, 0, 1, 3))


def solution(mesh):
    in_specs = (P("gz", "rows", None, None), P("gz", None, None), P("gz", "rows"), P())
    out_specs = (P("gz", "rows", None, None), P(None, "gz", "rows", None))
    return jax.shard_map(functools.partial(on_device, mesh.shape["gz"]), mesh=mesh, in_specs=in_specs, out_specs=out_specs, check_vma=False)
```

profile of v0, /device:TPU:0, one launch (start us, length us, event | category | flops | bytes accessed | tf_op | source)
XLA Modules:
  0.0 173.3 jit_solution(2454769065792950516)
XLA Ops:
  0.6 0.7 convert_bitcast_fusion.1
  1.3 0.1 copy.7
  1.4 0.8 convert_bitcast_fusion
  2.2 0.6 concatenate.3.off_in
  2.8 0.8 multiply_convert_fusion.compat_in
  3.6 1.8 %copy.8.desc = bf16[4,225,256]{2,1,0:T(8,128)(2,1)} copy(bf16[4,225,256]{2,0,1:T(4,128)(2,1)} %param.5) | data formatting | bytes 921600 | tf_op args[1]
  5.4 5.1 %bitcast_multiply_fusion.data = bf16[4,4,225,512]{3,2,1,0:T(8,128)(2,1)} fusion(bf16[4,4,225,512]{3,1,2,0:T(4,128)(2,1)} %param.4, bf16[4,4]{1,0:T(4,128)(2,1)S(1)} %copy.7), kind=kLoop, calls=%fused_computation | loop fusion | flops 1843200 | bytes 7372832 | tf_op jit(solution)/shard_map/mul | solution.py:252
  10.5 153.7 %mega.1 = (f32[4,225,4,512]{3,2,1,0:T(4,128)}, f32[4,4,8,512]{3,2,1,0:T(8,128)}) custom-call(bf16[4,4,225,512]{3,2,1,0:T(8,128)(2,1)} %bitcast_multiply_fusion.data, bf16[4,225,256]{2,1,0:T(8,128)(2,1)} %copy.8.desc, bf16[225,225]{1,0:T(8,128)(2,1)} %multiply_convert_fusion.compat_in, bf16[8,225]{1,0:T(8,128)(2,1)} %concatenate.3.off_in), custom_call_target="tpu_custom_call" | custom-call | tf_op jit(solution)/shard_map/mega/pallas_call | solution.py:258
  164.3 1.0 slice_bitcast_fusion
  165.2 0.6 copy.9
  165.9 7.4 %copy.12 = f32[4,4,225,512]{3,1,2,0:T(4,128)} copy(f32[4,4,225,512]{3,1,2,0:T(4,128)} %bitcast.11) | data formatting | bytes 14745600
  (1 shorter events, 0.0 us)
where the time goes:
time: 176 us; the launch traced here: 173 us
  Pallas kernels  154 us (88%)
  local copies, waits for them, and re-layouts  11.6 us (7%)
  other arithmetic  7.35 us (4%)
    pallas_call x1, Pallas kernels, on_device(): pl.pallas_call(functools.partial(kernel, n), in_specs=[hbm] * 4, out_spec...  154 us
    unnamed x3, local copies, waits for them, and re-layouts  9.91 us
    mul x1, other arithmetic, on_device(): jnp.transpose(unary_cost, (1, 0, 2, 3))  5.13 us

commit v1 on v0

v1 whole, which is shorter than its diff:
```python
import functools

import jax
import jax.numpy as jnp
from jax import lax
from jax.experimental import pallas as pl
from jax.experimental.pallas import tpu as pltpu
from jax.sharding import PartitionSpec as P

BF = jnp.bfloat16
F32 = jnp.float32
MESH = pl.DeviceIdType.MESH
LAB = 225
FEAT = 256
COLS = 512


def kernel(n, data, desc, compat_in, off_in, out, disp, x, xr, m0, m0r, p0, p0r, p1, m1, dd, dt, compat, off, s0, s1, ps0, ps1, stage, send, recv, load, store):
    d = lax.axis_index("gz")
    h = lax.axis_index("rows")
    par = lax.rem(d, 2)
    prev = lax.rem(d + n - 1, n)
    nxt = lax.rem(d + 1, n)
    other = 1 - h
    relay_to = lax.rem(d + n - 1 + 2 * par, n)
    swap_with = d + 1 - 2 * par
    r0 = 2 - 2 * h
    s_bufs = (s0, s1)
    ps_bufs = (ps0, ps1)
    r_edge = 3 - 3 * h
    below = jnp.where(d > 0, 1.0, 0.0).astype(F32)
    above = jnp.where(d < n - 1, 1.0, 0.0).astype(F32)

    def row(q):
        return q + h * (3 - 2 * q)

    barrier = pltpu.get_barrier_semaphore()
    for g in (prev, nxt):
        for k in (h, other):
            pl.semaphore_signal(barrier, inc=1, device_id=(g, k), device_id_type=MESH)
    pl.semaphore_wait(barrier, 4)

    count = [0]

    def remote(src, dst, g, k):
        i = count[0]
        count[0] += 1
        return pltpu.make_async_remote_copy(src_ref=src, dst_ref=dst, send_sem=send.at[i], recv_sem=recv.at[i], device_id=(g, k), device_id_type=MESH)

    def blocks(rows, up_s, up_e, dn_s, dn_e):
        return (
            remote(data.at[rows, pl.ds(up_s, 2)], x.at[rows, pl.ds(up_e, 2)], nxt, h),
            remote(data.at[rows, pl.ds(dn_s, 2)], x.at[rows, pl.ds(dn_e, 2)], prev, h),
        )

    edge_rows = pl.ds(r0, 2)
    near_edge = blocks(edge_rows, 2, 2, 0, 8)
    far_edge = blocks(edge_rows, 0, 0, 2, 10)
    near_rest = blocks(pl.ds(2 - r0, 2), 2, 2, 0, 8)
    far_one = blocks(pl.ds(row(1), 1), 0, 0, 2, 10)
    far_zero = blocks(pl.ds(row(0), 1), 0, 0, 2, 10)
    desc_up = remote(desc, dd.at[pl.ds(0, 4)], nxt, jnp.where(par == 0, h, other))
    desc_dn = remote(desc, dd.at[pl.ds(8, 4)], prev, jnp.where(par == 0, other, h))
    corner = remote(data.at[r_edge, pl.ds(2 * par, 2)], xr.at[other, pl.ds(6 - 6 * par, 2)], relay_to, other)
    relay_near = remote(x.at[edge_rows, pl.ds(2 + 6 * par, 2)], xr.at[:, pl.ds(4 - 2 * par, 2)], relay_to, other)
    relay_far = remote(x.at[edge_rows, pl.ds(10 * par, 2)], xr.at[:, pl.ds(2 + 2 * par, 2)], relay_to, other)
    swap = remote(xr.at[h, pl.ds(4 - 2 * par, 2)], xr.at[h, pl.ds(6 * par, 2)], swap_with, h)

    def start(*copies):
        for c in copies:
            c.start()

    def arrived(*copies):
        for c in copies:
            c.wait_recv()

    start(*near_edge, desc_up, desc_dn, corner)
    loads = [
        pltpu.make_async_copy(data, x.at[:, pl.ds(4, 4)], load.at[0]),
        pltpu.make_async_copy(desc, dd.at[pl.ds(4, 4)], load.at[1]),
        pltpu.make_async_copy(compat_in, compat, load.at[2]),
        pltpu.make_async_copy(off_in, off, load.at[3]),
    ]
    for c in loads:
        c.start()
    for c in loads:
        c.wait()

    def loop(count_, body):
        lax.fori_loop(0, count_, lambda i, c: (body(i), c)[1], 0)

    def soft_to(src, dst, flag):
        for j in range(4):
            cols = pl.ds(128 * j, 128)
            w = jnp.exp(-src[:, cols].astype(F32))
            inv = flag / jnp.sum(w, axis=0, keepdims=True)
            dst[:, cols] = (w * inv).astype(BF)

    def flag_of(e):
        return jnp.where(e < 4, below, jnp.where(e > 7, above, 1.0))

    def transpose(e):
        dt[e] = jnp.transpose(dd[e].astype(F32)).astype(BF)

    def project(e, src, dst):
        dst[...] = jnp.dot(dt[e], src[...], preferred_element_type=F32).astype(BF)

    lane512 = lax.broadcasted_iota(jnp.int32, (LAB, COLS), 1)

    def gather(near, far, planes, centre, s_buf):
        half = jnp.asarray(0.5, BF)
        cc = centre[...]
        lf = jnp.where(lane512 > 0, pltpu.roll(cc, 1, 1), jnp.zeros_like(cc))
        rt = jnp.where(lane512 < COLS - 1, pltpu.roll(cc, COLS - 1, 1), jnp.zeros_like(cc))
        lr = lf + rt
        for j in range(COLS // 256):
            cols = pl.ds(256 * j, 256)
            z = (near[0][:, cols] + near[1][:, cols]) + half * (far[0][:, cols] + far[1][:, cols])
            p = planes[0][:, cols]
            for q in planes[1:]:
                p = p + q[:, cols]
            s_buf[:, cols] = lr[:, 256 * j : 256 * j + 256] + p + z

    def gather_p(a, b, c, g, ps_buf):
        ps_buf[...] = (a[...] + b[...]) + (c[...] + g[...])

    def energy_of(e, dref, cols, s_buf, ps_buf):
        v = dref[:, cols].astype(F32)
        v = v + jnp.dot(compat[...], s_buf[:, cols], preferred_element_type=F32)
        return v + jnp.dot(dd[e], ps_buf[:, cols], preferred_element_type=F32)

    def norm(v, flag):
        w = jnp.exp(-v)
        inv = flag / jnp.sum(w, axis=0, keepdims=True)
        return (w * inv).astype(BF)

    def pairs(count_, *phases):
        def body(i):
            for phase in phases:
                for u in range(2):
                    phase(2 * i + u, u)
        loop(count_ // 2, body)

    def sweep1(q, at, count_):
        r = row(q)

        def collect(i, u):
            e = at(i)
            planes = []
            if q > 0:
                planes.append(m0.at[row(q - 1), e])
            planes.append(m0.at[row(q + 1), e] if q < 3 else m0r.at[e - 2])
            gather((m0.at[r, e - 1], m0.at[r, e + 1]), (m0.at[r, e - 2], m0.at[r, e + 2]), planes, m0.at[r, e], s_bufs[u])
            gather_p(p0.at[r, e - 1], p0.at[r, e + 1], p0.at[r, e - 2], p0.at[r, e + 2], ps_bufs[u])

        def settle(i, u):
            e = at(i)
            for j in range(2):
                cols = pl.ds(256 * j, 256)
                m1.at[r, e - 2][:, cols] = norm(energy_of(e, x.at[r, e], cols, s_bufs[u], ps_bufs[u]), flag_of(e))

        def forward(i, u):
            e = at(i)
            project(e, m1.at[r, e - 2], p1.at[r, e - 2])

        pairs(count_, collect, settle, forward)

    def sweep1_rim():
        def collect(i, u):
            e, t = 4 + i, 2 + i
            gather((m0r.at[t - 1], m0r.at[t + 1]), (m0r.at[t - 2], m0r.at[t + 2]), [m0.at[row(3), e], m0r.at[8 + i]], m0r.at[t], s_bufs[u])
            gather_p(p0r.at[t - 1], p0r.at[t + 1], p0r.at[t - 2], p0r.at[t + 2], ps_bufs[u])

        def settle(i, u):
            for j in range(2):
                cols = pl.ds(256 * j, 256)
                m0r.at[8 + i][:, cols] = norm(energy_of(4 + i, xr.at[h, 2 + i], cols, s_bufs[u], ps_bufs[u]), 1.0)

        pairs(4, collect, settle)

    def copy_out(r, k, u):
        return pltpu.make_async_copy(stage.at[u], out.at[k, :, r, :], store.at[u])

    def sweep2(q, first_use):
        r = row(q)

        def collect(k, u):
            t = 2 + k
            planes = []
            if q > 0:
                planes.append(m1.at[row(q - 1), t])
            planes.append(m1.at[row(q + 1), t] if q < 3 else m0r.at[8 + k])
            gather((m1.at[r, t - 1], m1.at[r, t + 1]), (m1.at[r, t - 2], m1.at[r, t + 2]), planes, m1.at[r, t], s_bufs[u])
            gather_p(p1.at[r, t - 1], p1.at[r, t + 1], p1.at[r, t - 2], p1.at[r, t + 2], ps_bufs[u])

        def settle(k, u):
            if first_use:
                @pl.when(k >= 2)
                def _():
                    copy_out(r, k, u).wait()
            else:
                copy_out(r, k, u).wait()
            for j in range(2):
                cols = pl.ds(256 * j, 256)
                v = energy_of(4 + k, x.at[r, 4 + k], cols, s_bufs[u], ps_bufs[u])
                stage.at[u][:, cols] = v
                disp.at[k, r][:, cols] = jnp.dot(off[...], norm(v, 1.0), preferred_element_type=F32)
            copy_out(r, k, u).start()

        pairs(4, collect, settle)

    def wing(i):
        return 2 + i + 4 * lax.div(i, 2)

    def tip(i):
        return i + 8 * lax.div(i, 2)

    def own(i):
        return 4 + i

    def first(count_, at):
        def soft(i, u):
            r, e = at(i)
            soft_to(x.at[r, e], m0.at[r, e], flag_of(e))

        def proj(i, u):
            r, e = at(i)
            project(e, m0.at[r, e], p0.at[r, e])

        pairs(count_, soft, proj)

    loop(4, lambda i: transpose(4 + i))
    first(16, lambda i: (lax.div(i, 4), 4 + lax.rem(i, 4)))

    arrived(*near_edge)
    start(*far_edge, relay_near)
    arrived(desc_up, desc_dn)
    loop(8, lambda i: transpose(i + 4 * lax.div(i, 4)))
    first(8, lambda i: (row(2 + lax.div(i, 4)), wing(lax.rem(i, 4))))
    sweep1(2, own, 4)
    arrived(*far_edge)
    start(*near_rest, relay_far)
    first(8, lambda i: (row(2 + lax.div(i, 4)), tip(lax.rem(i, 4))))
    arrived(corner, relay_near, relay_far)
    swap.start()
    arrived(swap)

    arrived(*near_rest)
    start(*far_one, *far_zero)
    first(8, lambda i: (row(lax.div(i, 4)), wing(lax.rem(i, 4))))

    def rim_soft(t, u):
        soft_to(xr.at[h, t], m0r.at[t], flag_of(t + 2))

    def rim_proj(t, u):
        project(t + 2, m0r.at[t], p0r.at[t])

    pairs(8, rim_soft, rim_proj)
    pairs(4, lambda i, u: soft_to(xr.at[other, i + 2], m0r.at[8 + i], 1.0))
    sweep1_rim()
    sweep1(3, lambda i: 2 + i, 8)
    sweep1(2, wing, 4)
    sweep1(1, own, 4)
    sweep1(0, own, 4)
    sweep2(3, True)
    sweep2(2, False)

    for q, copies in ((1, far_one), (0, far_zero)):
        arrived(*copies)
        first(4, lambda i: (row(q), tip(i)))
        sweep1(q, wing, 4)
        sweep2(q, False)
    for u in range(2):
        copy_out(row(0), u, u).wait()
    for c in (*near_edge, *far_edge, *near_rest, *far_one, *far_zero, desc_up, desc_dn, corner, relay_near, relay_far, swap):
        c.wait_send()


def on_device(n, unary_cost, descriptors, valid_rows, offsets):
    data = jnp.transpose(unary_cost, (1, 0, 2, 3)) * valid_rows.astype(BF).T[:, :, None, None]
    co = offsets.astype(F32)
    spread = jnp.abs(co[:, None, 0] - co[None, :, 0]) + jnp.abs(co[:, None, 1] - co[None, :, 1])
    compat = (0.125 * jnp.minimum(spread, 6.0)).astype(BF)
    off8 = jnp.concatenate([offsets.T, jnp.zeros((6, LAB), offsets.dtype)], axis=0).astype(BF)
    hbm = pl.BlockSpec(memory_space=pl.ANY)
    e, disp = pl.pallas_call(
        functools.partial(kernel, n),
        in_specs=[hbm] * 4,
        out_specs=[hbm, pl.BlockSpec(memory_space=pltpu.VMEM)],
        out_shape=[jax.ShapeDtypeStruct((4, LAB, 4, COLS), F32), jax.ShapeDtypeStruct((4, 4, 8, COLS), F32)],
        scratch_shapes=[
            pltpu.VMEM((4, 12, LAB, COLS), BF),
            pltpu.VMEM((2, 8, LAB, COLS), BF),
            pltpu.VMEM((4, 12, LAB, COLS), BF),
            pltpu.VMEM((12, LAB, COLS), BF),
            pltpu.VMEM((4, 12, FEAT, COLS), BF),
            pltpu.VMEM((8, FEAT, COLS), BF),
            pltpu.VMEM((4, 8, FEAT, COLS), BF),
            pltpu.VMEM((4, 8, LAB, COLS), BF),
            pltpu.VMEM((12, LAB, FEAT), BF),
            pltpu.VMEM((12, FEAT, LAB), BF),
            pltpu.VMEM((LAB, LAB), BF),
            pltpu.VMEM((8, LAB), BF),
            pltpu.VMEM((LAB, COLS), BF),
            pltpu.VMEM((LAB, COLS), BF),
            pltpu.VMEM((FEAT, COLS), BF),
            pltpu.VMEM((FEAT, COLS), BF),
            pltpu.VMEM((2, LAB, COLS), F32),
            pltpu.SemaphoreType.DMA((16,)),
            pltpu.SemaphoreType.DMA((16,)),
            pltpu.SemaphoreType.DMA((4,)),
            pltpu.SemaphoreType.DMA((2,)),
        ],
        compiler_params=pltpu.CompilerParams(collective_id=0, has_side_effects=True, vmem_limit_bytes=67043328),
        name="mega",
    )(data, descriptors, compat, off8)
    return jnp.transpose(e, (0, 2, 1, 3)), jnp.transpose(disp[:, :, 0:2], (2, 0, 1, 3))


def solution(mesh):
    in_specs = (P("gz", "rows", None, None), P("gz", None, None), P("gz", "rows"), P())
    out_specs = (P("gz", "rows", None, None), P(None, "gz", "rows", None))
    return jax.shard_map(functools.partial(on_device, mesh.shape["gz"]), mesh=mesh, in_specs=in_specs, out_specs=out_specs, check_vma=False)
```

time: 176 us -> 143 us (0.81)
  Pallas kernels: 154 us -> 122 us
    pallas_call x1, Pallas kernels: 154 us -> 122 us  [on_device(): pl.pallas_call(functools.partial(kernel, n), in_specs=[hbm] * 4, out_spec...]
where the time goes in v1:
time: 143 us; the launch traced here: 142 us
  Pallas kernels  122 us (85%)
  local copies, waits for them, and re-layouts  11.6 us (8%)
  other arithmetic  7.35 us (5%)
    pallas_call x1, Pallas kernels, on_device(): pl.pallas_call(functools.partial(kernel, n), in_specs=[hbm] * 4, out_spec...  122 us
    unnamed x3, local copies, waits for them, and re-layouts  9.91 us
    mul x1, other arithmetic, on_device(): jnp.transpose(unary_cost, (1, 0, 2, 3))  5.13 us

profile of v1, /device:TPU:0, one launch (start us, length us, event | category | flops | bytes accessed | tf_op | source)
XLA Modules:
  0.0 141.8 jit_solution(13028310646551521136)
XLA Ops:
  0.6 0.7 convert_bitcast_fusion.1
  1.3 0.1 copy.7
  1.4 0.8 convert_bitcast_fusion
  2.2 0.6 concatenate.3.off_in
  2.8 0.8 multiply_convert_fusion.compat_in
  3.6 1.8 %copy.8.desc = bf16[4,225,256]{2,1,0:T(8,128)(2,1)} copy(bf16[4,225,256]{2,0,1:T(4,128)(2,1)} %param.5) | data formatting | bytes 921600 | tf_op args[1]
  5.4 5.1 %bitcast_multiply_fusion.data = bf16[4,4,225,512]{3,2,1,0:T(8,128)(2,1)} fusion(bf16[4,4,225,512]{3,1,2,0:T(4,128)(2,1)} %param.4, bf16[4,4]{1,0:T(4,128)(2,1)S(1)} %copy.7), kind=kLoop, calls=%fused_computation | loop fusion | flops 1843200 | bytes 7372832 | tf_op jit(solution)/shard_map/mul | solution.py:280
  10.5 122.2 %mega.1 = (f32[4,225,4,512]{3,2,1,0:T(4,128)}, f32[4,4,8,512]{3,2,1,0:T(8,128)}) custom-call(bf16[4,4,225,512]{3,2,1,0:T(8,128)(2,1)} %bitcast_multiply_fusion.data, bf16[4,225,256]{2,1,0:T(8,128)(2,1)} %copy.8.desc, bf16[225,225]{1,0:T(8,128)(2,1)} %multiply_convert_fusion.compat_in, bf16[8,225]{1,0:T(8,128)(2,1)} %concatenate.3.off_in), custom_call_target="tpu_custom_call" | custom-call | tf_op jit(solution)/shard_map/mega/pallas_call | solution.py:286
  132.8 1.0 slice_bitcast_fusion
  133.7 0.6 copy.9
  134.4 7.4 %copy.12 = f32[4,4,225,512]{3,1,2,0:T(4,128)} copy(f32[4,4,225,512]{3,1,2,0:T(4,128)} %bitcast.11) | data formatting | bytes 14745600
  (1 shorter events, 0.0 us)

commit v2 on v1

--- a/solution.py
+++ b/solution.py
@@ -15,7 +15,7 @@
 COLS = 512
 
 
-def kernel(n, data, desc, compat_in, off_in, out, disp, x, xr, m0, m0r, p0, p0r, p1, m1, dd, dt, compat, off, s0, s1, ps0, ps1, stage, send, recv, load, store):
+def kernel(n, data, desc, off_in, out, disp, x, xr, m0, m0r, p0, p0r, p1, m1, dd, dt, compat, off, s0, s1, ps0, ps1, stage, send, recv, load, store):
     d = lax.axis_index("gz")
     h = lax.axis_index("rows")
     par = lax.rem(d, 2)
@@ -56,14 +56,16 @@
     edge_rows = pl.ds(r0, 2)
     near_edge = blocks(edge_rows, 2, 2, 0, 8)
     far_edge = blocks(edge_rows, 0, 0, 2, 10)
-    near_rest = blocks(pl.ds(2 - r0, 2), 2, 2, 0, 8)
+    near_one = blocks(pl.ds(row(1), 1), 2, 2, 0, 8)
+    near_zero = blocks(pl.ds(row(0), 1), 2, 2, 0, 8)
     far_one = blocks(pl.ds(row(1), 1), 0, 0, 2, 10)
     far_zero = blocks(pl.ds(row(0), 1), 0, 0, 2, 10)
     desc_up = remote(desc, dd.at[pl.ds(0, 4)], nxt, jnp.where(par == 0, h, other))
     desc_dn = remote(desc, dd.at[pl.ds(8, 4)], prev, jnp.where(par == 0, other, h))
     corner = remote(data.at[r_edge, pl.ds(2 * par, 2)], xr.at[other, pl.ds(6 - 6 * par, 2)], relay_to, other)
     relay_near = remote(x.at[edge_rows, pl.ds(2 + 6 * par, 2)], xr.at[:, pl.ds(4 - 2 * par, 2)], relay_to, other)
-    relay_far = remote(x.at[edge_rows, pl.ds(10 * par, 2)], xr.at[:, pl.ds(2 + 2 * par, 2)], relay_to, other)
+    relay_far = remote(x.at[r_edge, pl.ds(10 * par, 2)], xr.at[other, pl.ds(2 + 2 * par, 2)], relay_to, other)
+    relay_last = remote(x.at[row(2), pl.ds(10 * par, 2)], xr.at[h, pl.ds(2 + 2 * par, 2)], relay_to, other)
     swap = remote(xr.at[h, pl.ds(4 - 2 * par, 2)], xr.at[h, pl.ds(6 * par, 2)], swap_with, h)
 
     def start(*copies):
@@ -78,8 +80,6 @@
     loads = [
         pltpu.make_async_copy(data, x.at[:, pl.ds(4, 4)], load.at[0]),
         pltpu.make_async_copy(desc, dd.at[pl.ds(4, 4)], load.at[1]),
-        pltpu.make_async_copy(compat_in, compat, load.at[2]),
-        pltpu.make_async_copy(off_in, off, load.at[3]),
     ]
     for c in loads:
         c.start()
@@ -204,7 +204,7 @@
                 cols = pl.ds(256 * j, 256)
                 v = energy_of(4 + k, x.at[r, 4 + k], cols, s_bufs[u], ps_bufs[u])
                 stage.at[u][:, cols] = v
-                disp.at[k, r][:, cols] = jnp.dot(off[...], norm(v, 1.0), preferred_element_type=F32)
+                disp.at[k, r][:, cols] = jnp.dot(off[...].astype(BF), norm(v, 1.0), preferred_element_type=F32)
             copy_out(r, k, u).start()
 
         pairs(4, collect, settle)
@@ -229,39 +229,55 @@
 
         pairs(count_, soft, proj)
 
+    off[...] = jnp.concatenate([off_in[...].astype(F32), jnp.zeros((6, LAB), F32)], axis=0)
+    turned = jnp.transpose(off[...])
+    spread = jnp.abs(turned[:, 0:1] - off[0:1, :]) + jnp.abs(turned[:, 1:2] - off[1:2, :])
+    compat[...] = (0.125 * jnp.minimum(spread, 6.0)).astype(BF)
+
     loop(4, lambda i: transpose(4 + i))
     first(16, lambda i: (lax.div(i, 4), 4 + lax.rem(i, 4)))
 
+    half = 4 * par
+
+    def rim(slot):
+        def rim_soft(i, u):
+            soft_to(xr.at[h, slot + i], m0r.at[slot + i], flag_of(slot + i + 2))
+
+        def rim_proj(i, u):
+            project(slot + i + 2, m0r.at[slot + i], p0r.at[slot + i])
+
+        pairs(4, rim_soft, rim_proj)
+        sweep1(3, lambda i: 2 + slot + i, 4)
+
+    start(*far_edge)
     arrived(*near_edge)
-    start(*far_edge, relay_near)
+    start(relay_near)
     arrived(desc_up, desc_dn)
     loop(8, lambda i: transpose(i + 4 * lax.div(i, 4)))
     first(8, lambda i: (row(2 + lax.div(i, 4)), wing(lax.rem(i, 4))))
     sweep1(2, own, 4)
+    start(*near_one)
     arrived(*far_edge)
-    start(*near_rest, relay_far)
+    start(relay_far, *near_zero)
     first(8, lambda i: (row(2 + lax.div(i, 4)), tip(lax.rem(i, 4))))
-    arrived(corner, relay_near, relay_far)
-    swap.start()
-    arrived(swap)
-
-    arrived(*near_rest)
-    start(*far_one, *far_zero)
-    first(8, lambda i: (row(lax.div(i, 4)), wing(lax.rem(i, 4))))
-
-    def rim_soft(t, u):
-        soft_to(xr.at[h, t], m0r.at[t], flag_of(t + 2))
-
-    def rim_proj(t, u):
-        project(t + 2, m0r.at[t], p0r.at[t])
-
-    pairs(8, rim_soft, rim_proj)
+
+    arrived(*near_one)
+    start(*far_one)
+    first(4, lambda i: (row(1), wing(i)))
+    sweep1(2, wing, 4)
+    arrived(relay_far)
+    start(swap, relay_last)
+    sweep1(1, own, 4)
+    arrived(corner, relay_near)
+    rim(half)
+    arrived(*near_zero)
+    start(*far_zero)
+    first(4, lambda i: (row(0), wing(i)))
+    sweep1(0, own, 4)
+    arrived(swap, relay_last)
+    rim(4 - half)
     pairs(4, lambda i, u: soft_to(xr.at[other, i + 2], m0r.at[8 + i], 1.0))
     sweep1_rim()
-    sweep1(3, lambda i: 2 + i, 8)
-    sweep1(2, wing, 4)
-    sweep1(1, own, 4)
-    sweep1(0, own, 4)
     sweep2(3, True)
     sweep2(2, False)
 
@@ -272,20 +288,16 @@
         sweep2(q, False)
     for u in range(2):
         copy_out(row(0), u, u).wait()
-    for c in (*near_edge, *far_edge, *near_rest, *far_one, *far_zero, desc_up, desc_dn, corner, relay_near, relay_far, swap):
+    for c in (*near_edge, *far_edge, *near_one, *near_zero, *far_one, *far_zero, desc_up, desc_dn, corner, relay_near, relay_far, relay_last, swap):
         c.wait_send()
 
 
 def on_device(n, unary_cost, descriptors, valid_rows, offsets):
     data = jnp.transpose(unary_cost, (1, 0, 2, 3)) * valid_rows.astype(BF).T[:, :, None, None]
-    co = offsets.astype(F32)
-    spread = jnp.abs(co[:, None, 0] - co[None, :, 0]) + jnp.abs(co[:, None, 1] - co[None, :, 1])
-    compat = (0.125 * jnp.minimum(spread, 6.0)).astype(BF)
-    off8 = jnp.concatenate([offsets.T, jnp.zeros((6, LAB), offsets.dtype)], axis=0).astype(BF)
     hbm = pl.BlockSpec(memory_space=pl.ANY)
     e, disp = pl.pallas_call(
         functools.partial(kernel, n),
-        in_specs=[hbm] * 4,
+        in_specs=[hbm, hbm, pl.BlockSpec(memory_space=pltpu.VMEM)],
         out_specs=[hbm, pl.BlockSpec(memory_space=pltpu.VMEM)],
         out_shape=[jax.ShapeDtypeStruct((4, LAB, 4, COLS), F32), jax.ShapeDtypeStruct((4, 4, 8, COLS), F32)],
         scratch_shapes=[
@@ -300,20 +312,20 @@
             pltpu.VMEM((12, LAB, FEAT), BF),
             pltpu.VMEM((12, FEAT, LAB), BF),
             pltpu.VMEM((LAB, LAB), BF),
-            pltpu.VMEM((8, LAB), BF),
+            pltpu.VMEM((8, LAB), F32),
             pltpu.VMEM((LAB, COLS), BF),
             pltpu.VMEM((LAB, COLS), BF),
             pltpu.VMEM((FEAT, COLS), BF),
             pltpu.VMEM((FEAT, COLS), BF),
             pltpu.VMEM((2, LAB, COLS), F32),
-            pltpu.SemaphoreType.DMA((16,)),
-            pltpu.SemaphoreType.DMA((16,)),
-            pltpu.SemaphoreType.DMA((4,)),
+            pltpu.SemaphoreType.DMA((19,)),
+            pltpu.SemaphoreType.DMA((19,)),
+            pltpu.SemaphoreType.DMA((2,)),
             pltpu.SemaphoreType.DMA((2,)),
         ],
         compiler_params=pltpu.CompilerParams(collective_id=0, has_side_effects=True, vmem_limit_bytes=67043328),
         name="mega",
-    )(data, descriptors, compat, off8)
+    )(data, descriptors, offsets.T)
     return jnp.transpose(e, (0, 2, 1, 3)), jnp.transpose(disp[:, :, 0:2], (2, 0, 1, 3))
 
 

time: 143 us -> 131 us (0.916)
  Pallas kernels: 122 us -> 114 us
  other arithmetic: 7.35 us -> 5.82 us
    pallas_call x1, Pallas kernels: 122 us -> 114 us  [on_device(): pl.pallas_call(functools.partial(kernel, n), in_specs=[hbm, hbm, pl.Block...]
where the time goes in v2:
time: 131 us
  Pallas kernels  114 us (87%)
  local copies, waits for them, and re-layouts  11 us (8%)
  other arithmetic  5.82 us (4%)
    pallas_call x1, Pallas kernels, on_device(): pl.pallas_call(functools.partial(kernel, n), in_specs=[hbm, hbm, pl.Block...  114 us
    unnamed x3, local copies, waits for them, and re-layouts  9.92 us
    mul x1, other arithmetic, on_device(): jnp.transpose(unary_cost, (1, 0, 2, 3))  5.13 us

profile of v2, /device:TPU:0, one launch (start us, length us, event | category | flops | bytes accessed | tf_op | source)
XLA Modules:
  0.0 131.0 jit_solution(12055393440743400693)
XLA Ops:
  0.6 0.7 convert_bitcast_fusion
  1.3 0.1 copy.7
  1.4 1.9 %copy.8.desc = bf16[4,225,256]{2,1,0:T(8,128)(2,1)} copy(bf16[4,225,256]{2,0,1:T(4,128)(2,1)} %param.5) | data formatting | bytes 921600 | tf_op args[1]
  3.3 5.1 %bitcast_multiply_fusion.data = bf16[4,4,225,512]{3,2,1,0:T(8,128)(2,1)} fusion(bf16[4,4,225,512]{3,1,2,0:T(4,128)(2,1)} %param.4, bf16[4,4]{1,0:T(4,128)(2,1)S(1)} %copy.7), kind=kLoop, calls=%fused_computation | loop fusion | flops 1843200 | bytes 7372832 | tf_op jit(solution)/shard_map/mul | solution.py:296
  8.4 113.5 %mega.1 = (f32[4,225,4,512]{3,2,1,0:T(4,128)}, f32[4,4,8,512]{3,2,1,0:T(8,128)}) custom-call(bf16[4,4,225,512]{3,2,1,0:T(8,128)(2,1)} %bitcast_multiply_fusion.data, bf16[4,225,256]{2,1,0:T(8,128)(2,1)} %copy.8.desc, s32[2,225]{1,0:T(2,128)} %bitcast.9), custom_call_target="tpu_custom_call" | custom-call | tf_op jit(solution)/shard_map/mega/pallas_call | solution.py:298
  121.9 1.0 slice_bitcast_fusion
  122.9 0.6 copy.9
  123.6 7.4 %copy.12 = f32[4,4,225,512]{3,1,2,0:T(4,128)} copy(f32[4,4,225,512]{3,1,2,0:T(4,128)} %bitcast.8) | data formatting | bytes 14745600

commit v3 on v2

--- a/solution.py
+++ b/solution.py
@@ -204,7 +204,9 @@
                 cols = pl.ds(256 * j, 256)
                 v = energy_of(4 + k, x.at[r, 4 + k], cols, s_bufs[u], ps_bufs[u])
                 stage.at[u][:, cols] = v
-                disp.at[k, r][:, cols] = jnp.dot(off[...].astype(BF), norm(v, 1.0), preferred_element_type=F32)
+                mean = jnp.dot(off[...].astype(BF), norm(v, 1.0), preferred_element_type=F32)
+                for axis in range(2):
+                    disp[axis, k, pl.ds(r, 1), cols] = mean[axis : axis + 1]
             copy_out(r, k, u).start()
 
         pairs(4, collect, settle)
@@ -299,7 +301,7 @@
         functools.partial(kernel, n),
         in_specs=[hbm, hbm, pl.BlockSpec(memory_space=pltpu.VMEM)],
         out_specs=[hbm, pl.BlockSpec(memory_space=pltpu.VMEM)],
-        out_shape=[jax.ShapeDtypeStruct((4, LAB, 4, COLS), F32), jax.ShapeDtypeStruct((4, 4, 8, COLS), F32)],
+        out_shape=[jax.ShapeDtypeStruct((4, LAB, 4, COLS), F32), jax.ShapeDtypeStruct((2, 4, 4, COLS), F32)],
         scratch_shapes=[
             pltpu.VMEM((4, 12, LAB, COLS), BF),
             pltpu.VMEM((2, 8, LAB, COLS), BF),
@@ -326,7 +328,7 @@
         compiler_params=pltpu.CompilerParams(collective_id=0, has_side_effects=True, vmem_limit_bytes=67043328),
         name="mega",
     )(data, descriptors, offsets.T)
-    return jnp.transpose(e, (0, 2, 1, 3)), jnp.transpose(disp[:, :, 0:2], (2, 0, 1, 3))
+    return jnp.transpose(e, (0, 2, 1, 3)), disp
 
 
 def solution(mesh):

time: 131 us -> 130 us (level)
    unnamed x3 -> x5, local copies, waits for them, and re-layouts: 9.92 us -> 9.93 us
where the time goes in v3:
time: 130 us
  Pallas kernels  114 us (88%)
  local copies, waits for them, and re-layouts  10 us (8%)
  other arithmetic  5.82 us (4%)
    pallas_call x1, Pallas kernels, on_device(): pl.pallas_call(functools.partial(kernel, n), in_specs=[hbm, hbm, pl.Block...  114 us
    unnamed x5, local copies, waits for them, and re-layouts  9.93 us
    mul x1, other arithmetic, on_device(): jnp.transpose(unary_cost, (1, 0, 2, 3))  5.13 us

profile of v3, /device:TPU:0, one launch (start us, length us, event | category | flops | bytes accessed | tf_op | source)
XLA Modules:
  0.0 130.0 jit_solution(5600822060557555971)
XLA Ops:
  0.6 0.7 convert_bitcast_fusion
  1.3 0.1 copy.7
  1.4 1.8 %copy.8.desc = bf16[4,225,256]{2,1,0:T(8,128)(2,1)} copy(bf16[4,225,256]{2,0,1:T(4,128)(2,1)} %param.5) | data formatting | bytes 921600 | tf_op args[1]
  3.3 5.1 %bitcast_multiply_fusion.data = bf16[4,4,225,512]{3,2,1,0:T(8,128)(2,1)} fusion(bf16[4,4,225,512]{3,1,2,0:T(4,128)(2,1)} %param.4, bf16[4,4]{1,0:T(4,128)(2,1)S(1)} %copy.7), kind=kLoop, calls=%fused_computation | loop fusion | flops 1843200 | bytes 7372832 | tf_op jit(solution)/shard_map/mul | solution.py:298
  8.4 113.5 %mega.1 = (f32[4,225,4,512]{3,2,1,0:T(4,128)}, f32[2,4,4,512]{3,2,1,0:T(4,128)}) custom-call(bf16[4,4,225,512]{3,2,1,0:T(8,128)(2,1)} %bitcast_multiply_fusion.data, bf16[4,225,256]{2,1,0:T(8,128)(2,1)} %copy.8.desc, s32[2,225]{1,0:T(2,128)} %bitcast.7), custom_call_target="tpu_custom_call" | custom-call | tf_op jit(solution)/shard_map/mega/pallas_call | solution.py:300
  121.9 0.0 copy-start
  121.9 7.4 %copy.12 = f32[4,4,225,512]{3,1,2,0:T(4,128)} copy(f32[4,4,225,512]{3,1,2,0:T(4,128)} %bitcast.6) | data formatting | bytes 14745600
  129.4 0.0 copy-done
  129.4 0.6 copy.13
Async XLA Ops:
  121.9 7.5 %copy-start = (f32[2,4,4,512]{3,2,1,0:T(4,128)S(1)}, f32[2,4,4,512]{3,2,1,0:T(4,128)}, u32[]{:S(2)}) copy-start(f32[2,4,4,512]{3,2,1,0:T(4,128)} %get-tuple-element.9) | copy-start | bytes 196612
